TPU v7x, 128 devices: a whole 4x4x4 slice. The times are simulated.
128 devices in a mesh: gr: 16 (over x, y), gc: 8 (over z, core).
Axes of the slice: x: 4, y: 4, z: 4, core: 2. Of those that a mesh axis runs over, the one named last changes fastest.
Arguments:
- child_rows: float32 [8192, 12288], P('gr', 'gc'), may hold values from -1.5 to 1.5
- row_map: int32 [8192], P('gr'), may hold values from 0 to 8191, as said below
- stair: int32 [64], replicated, may hold values from 0 to 896, as said below
Outputs:
- factor: float32 [1024, 12288], P('gr', 'gc')
- projected: float32 [8192, 12288], P('gr', 'gc')
Inputs may be any that keep to these rules, and one draw needn't show every extreme that they name: row_map is a permutation of 0 to 8191. Of the 512 rows of one index of gr, at most 152 go to the rows of any one index of gr (row_map // 512), and some index of gr sends exactly 152 to one index. stair is nondecreasing and a multiple of 128; the first quarter of the blocks is 0 and the last block holds 896.
All inputs are finite; a program needn't handle non-finite values.
Results may differ from a plain program's by a relative error of at most 0.0003.
Values sent between devices are 32-bit elements; how exact they have to be, the bound alone decides.
A program may use at most 128 MiB of HBM per device.

v0:
```python
import jax
import jax.numpy as jnp
from jax import lax
from jax.sharding import PartitionSpec as P

PANEL = 512
NPANEL = 2
STAIR_BLOCK = 128


def spread(value, axis, source):
    kept = jnp.where(lax.axis_index(axis) == source, value, 0).astype(value.dtype)
    return lax.psum(kept, axis)


def pack_rows(values, targets, groups):
    rows_dev = values.shape[0]
    base_rows = 3 * rows_dev // (4 * groups)
    capacity = rows_dev - base_rows * (groups - 1)
    target_dev = targets // rows_dev
    target_row = targets % rows_dev
    onehot = (target_dev[:, None] == jnp.arange(groups, dtype=jnp.int32)[None, :]).astype(jnp.int32)
    rank_within = jnp.sum((jnp.cumsum(onehot, axis=0) - onehot) * onehot, axis=1)
    buffer_index = target_dev * capacity + rank_within
    source_row = (
        jnp.full((groups * capacity,), rows_dev, jnp.int32)
        .at[buffer_index]
        .set(jnp.arange(rows_dev, dtype=jnp.int32))
    )
    sent_rows = jnp.take(values, source_row, axis=0, mode="fill", fill_value=0.0)
    sent_slots = (
        jnp.full((groups * capacity,), rows_dev, jnp.int32).at[buffer_index].set(target_row)
    )
    return (
        sent_rows.reshape(groups, capacity, values.shape[1]),
        sent_slots.reshape(groups, capacity),
    )


def place_rows(recv_rows, recv_slots, rows_dev):
    flat_rows = recv_rows.reshape(-1, recv_rows.shape[-1])
    flat_slots = recv_slots.reshape(-1)
    where_from = (
        jnp.zeros((rows_dev,), jnp.int32)
        .at[flat_slots]
        .set(jnp.arange(flat_slots.shape[0], dtype=jnp.int32), mode="drop")
    )
    return jnp.take(flat_rows, where_from, axis=0)


def matmul(left, right):
    return jnp.dot(left, right, precision=lax.Precision.HIGHEST, preferred_element_type=jnp.float32)


def high(left, right, contract):
    return lax.dot_general(
        left,
        right,
        (contract, ((), ())),
        precision=lax.Precision.HIGH,
        preferred_element_type=jnp.float32,
    )


def cholesky_inverse(gram):
    lower = jnp.linalg.cholesky(gram)
    eye = jnp.eye(gram.shape[0], dtype=gram.dtype)
    return jax.scipy.linalg.solve_triangular(lower, eye, lower=True)


def gram_inverse_factor(g00, g10, g11):
    i00 = cholesky_inverse(g00)
    l10 = matmul(g10, i00.T)
    i11 = cholesky_inverse(g11 - matmul(l10, l10.T))
    i10 = -matmul(i11, matmul(l10, i00))
    return jnp.concatenate(
        [jnp.concatenate([i00, jnp.zeros_like(i00)], 1), jnp.concatenate([i10, i11], 1)], 0
    )


def shards(child_rows, row_map, stair):
    groups = lax.axis_size("gr")
    rows_dev, cols_dev = child_rows.shape
    wide = NPANEL * PANEL
    half = PANEL // 2
    columns = lax.axis_index("gc") * cols_dev + jnp.arange(cols_dev, dtype=jnp.int32)
    limits = jnp.take(stair, row_map // STAIR_BLOCK)
    masked = jnp.where(columns[None, :] >= limits[:, None], child_rows, jnp.zeros_like(child_rows))
    own = masked[:, :wide]
    left = matmul(own.T, own[:, :PANEL])
    low = matmul(own[:, PANEL:].T, own[:, PANEL:])
    low = jnp.concatenate([low[:, :half], low[:, half:]], axis=0)
    gram = jnp.concatenate([left, low], axis=1)
    gram = jnp.where(lax.axis_index("gc") == 0, gram, jnp.zeros_like(gram))
    gram, masked, own = lax.optimization_barrier((gram, masked, own))
    gram = lax.psum(gram, ("gr", "gc"))
    sent_rows, sent_slots = pack_rows(masked, row_map, groups)
    recv_rows, recv_slots = (
        lax.all_to_all(sent_rows, "gr", split_axis=0, concat_axis=0, tiled=True),
        lax.all_to_all(sent_slots, "gr", split_axis=0, concat_axis=0, tiled=True),
    )
    own, gram = lax.optimization_barrier((own, gram))
    panel = spread(own, "gc", 0)
    local = high(panel, masked, ((0,), (0,)))
    products = lax.psum(local, "gr")
    low = jnp.concatenate([gram[:PANEL, PANEL:], gram[PANEL:, PANEL:]], axis=1)
    inverse = gram_inverse_factor(gram[:PANEL, :PANEL], gram[PANEL:, :PANEL], low)
    front = place_rows(recv_rows, recv_slots, rows_dev)
    front_own, _ = lax.optimization_barrier((front[:, :wide], local))
    front_panel = spread(front_own, "gc", 0)
    basis = high(front_panel, inverse, ((1,), (1,)))
    stacked = high(inverse, products, ((1,), (0,)))
    projected = front - high(basis, stacked, ((1,), (0,)))
    share_rows = wide // groups
    factor = lax.dynamic_slice_in_dim(stacked, lax.axis_index("gr") * share_rows, share_rows, 0)
    return (factor, projected)


def solution(mesh):
    placed = (P("gr", "gc"), P("gr"), P())
    return jax.shard_map(
        shards,
        mesh=mesh,
        in_specs=placed,
        out_specs=(P("gr", "gc"), P("gr", "gc")),
        check_vma=False,
    )
```

profile of v0, /device:TPU:1, one launch (start us, length us, event | category | flops | bytes accessed | tf_op | source)
XLA Modules:
  0.0 959.6 jit_solution(5072844450119974676)
XLA Ops:
  28.0 40.5 %select_select_fusion.2 = s32[512]{0:T(512)S(1)} fusion(s32[512]{0:T(512)} %param.7, s32[]{:T(128)} %bitcast, s32[]{:T(128)} %bitcast.1, s32[]{:T(128)} %bitcast.2, s32[]{:T(128)} %bitcast.3, s32[]{:T(128)} %bitcast.4, s32[]{:T(128)} %bitcast.5, s32[]{:T(128)} %bitcast.6, s32[]{:T(128)} %bitcast.7, s32[]{:T(128)} %bitcast.8, s32[]{:T(128)} %bitcast.9, ...), kind=kLoop, calls=%fused_computation.171 | loop fusion | flops 75776 | bytes 4352 | tf_op jit(solution)/shard_map/jit(_take)/select_n | solution.py:87
  84.9 10.1 %gather_fusion = f32[2432,1536]{1,0:T(8,128)} fusion(f32[512,1536]{1,0:T(8,128)S(1)} %compare_select_fusion, s32[3072]{0:T(1024)S(1)} %pad_clamp_fusion), kind=kCustom, calls=%fused_computation | custom fusion | bytes 29894144 | tf_op jit(solution)/shard_map/jit(_take)/gather | solution.py:30
  95.0 11.6 %broadcast_select_fusion = f32[16,152,1536]{2,1,0:T(8,128)} fusion(f32[16,152,1536]{2,1,0:T(8,128)} %bitcast.192, pred[16,152]{1,0:T(8,128)(4,1)S(1)} %broadcast_in_dim.63), kind=kLoop, calls=%fused_computation.9 | loop fusion | flops 3735552 | bytes 29886848 | tf_op jit(solution)/shard_map/jit(_take)/select_n | solution.py:30
  114.4 12.8 %scatter_custom_fusion.1 = s32[512]{0:T(512)S(1)} fusion(s32[2432]{0:T(1024)S(1)} %fusion.76, s32[2432]{0:T(1024)S(1)} %iota.96, s32[]{:T(128)} %copy.55), kind=kCustom, calls=%fused_computation.190 | custom fusion | bytes 2052 | tf_op jit(solution)/shard_map/scatter | solution.py:46
  127.3 373.6 %all-reduce.7.cloned.1.call-done = f32[1024,768]{0,1:T(8,128)} async-done(((f32[1024,768]{0,1:T(8,128)}), f32[1024,768]{0,1:T(8,128)}) %all-reduce.7.cloned.1.call-update) | async-done | bytes 3145744 | tf_op jit(solution)/shard_map/psum | solution.py:96
  503.9 11.7 %cholesky.286 = f32[128,128]{1,0:T(8,128)S(1)} custom-call(f32[128,128]{1,0:T(8,128)S(1)} %cholesky.426), custom_call_target="Cholesky" | custom-call | tf_op jit(solution)/shard_map/jit(cholesky)/cholesky | solution.py:66
  516.8 9.8 %custom-call.27 = f32[1,128,128]{1,2,0:T(8,128)S(1)} custom-call(f32[1,128,128]{2,1,0:T(8,128)S(1)} %get-tuple-element.75), custom_call_target="InvertDiagBlocksLowerTriangular" | custom-call | tf_op jit(solution)/shard_map/jit(cholesky)/cholesky | solution.py:66
  529.0 11.7 %cholesky.305 = f32[128,128]{1,0:T(8,128)S(1)} custom-call(f32[128,128]{1,0:T(8,128)S(1)} %cholesky.430), custom_call_target="Cholesky" | custom-call | tf_op jit(solution)/shard_map/jit(cholesky)/cholesky | solution.py:66
  541.4 10.0 %custom-call.28 = f32[1,128,128]{1,2,0:T(8,128)S(1)} custom-call(f32[1,128,128]{2,1,0:T(8,128)S(1)} %get-tuple-element.72), custom_call_target="InvertDiagBlocksLowerTriangular" | custom-call | tf_op jit(solution)/shard_map/jit(cholesky)/cholesky | solution.py:66
  553.7 11.7 %cholesky.326 = f32[128,128]{1,0:T(8,128)S(1)} custom-call(f32[128,128]{1,0:T(8,128)S(1)} %cholesky.435), custom_call_target="Cholesky" | custom-call | tf_op jit(solution)/shard_map/jit(cholesky)/cholesky | solution.py:66
  578.2 11.7 %cholesky.343 = f32[128,128]{1,0:T(8,128)S(1)} custom-call(f32[128,128]{1,0:T(8,128)S(1)} %convolution_subtract_fusion.13), custom_call_target="Cholesky" | custom-call | tf_op jit(solution)/shard_map/jit(cholesky)/cholesky | solution.py:66
  597.7 11.8 %while.4 = (s32[]{:T(128)}, f32[512,512]{1,0:T(8,128)}, s32[4,2]{0,1:T(2,128)S(1)}, f32[4,128,128]{2,1,0:T(8,128)S(1)}, s32[]{:T(128)}) while((s32[]{:T(128)}, f32[512,512]{1,0:T(8,128)}, s32[4,2]{0,1:T(2,128)S(1)}, f32[4,128,128]{2,1,0:T(8,128)S(1)}, s32[]{:T(128)}) %tuple.124), condition=%wide.while_cond, body=%wide.while_body.sunk | while | flops 2 | bytes 131181 | solution.py:68
  609.5 39.9 %custom-call.30 = f32[4,128,128]{1,2,0:T(8,128)} custom-call(f32[4,128,128]{2,1,0:T(8,128)S(1)} %get-tuple-element.30), custom_call_target="InvertDiagBlocksLowerTriangular" | custom-call | tf_op jit(solution)/shard_map/jit(_solve_triangular)/triangular_solve | solution.py:68
  668.2 45.4 %all-reduce.9.cloned.1.call-done = f32[512,1024]{1,0:T(8,128)} async-done(((f32[512,1024]{1,0:T(8,128)}), f32[512,1024]{1,0:T(8,128)}) %all-reduce.9.cloned.1.call-update) | async-done | bytes 2097168 | tf_op jit(solution)/shard_map/psum | solution.py:13
  739.4 11.7 %cholesky.358 = f32[128,128]{1,0:T(8,128)S(1)} custom-call(f32[128,128]{1,0:T(8,128)S(1)} %cholesky.439), custom_call_target="Cholesky" | custom-call | tf_op jit(solution)/shard_map/jit(cholesky)/cholesky | solution.py:66
  766.0 11.7 %cholesky.377 = f32[128,128]{1,0:T(8,128)S(1)} custom-call(f32[128,128]{1,0:T(8,128)S(1)} %cholesky.443), custom_call_target="Cholesky" | custom-call | tf_op jit(solution)/shard_map/jit(cholesky)/cholesky | solution.py:66
  778.3 10.0 %custom-call.32 = f32[1,128,128]{1,2,0:T(8,128)S(1)} custom-call(f32[1,128,128]{2,1,0:T(8,128)S(1)} %get-tuple-element.62), custom_call_target="InvertDiagBlocksLowerTriangular" | custom-call | tf_op jit(solution)/shard_map/jit(cholesky)/cholesky | solution.py:66
  792.2 13.2 %cholesky.398 = f32[128,128]{1,0:T(8,128)} custom-call(f32[128,128]{1,0:T(8,128)} %cholesky.448), custom_call_target="Cholesky" | custom-call | tf_op jit(solution)/shard_map/jit(cholesky)/cholesky | solution.py:66
  806.9 11.3 %custom-call.33 = f32[1,128,128]{1,2,0:T(8,128)} custom-call(f32[1,128,128]{2,1,0:T(8,128)} %get-tuple-element.59), custom_call_target="InvertDiagBlocksLowerTriangular" | custom-call | tf_op jit(solution)/shard_map/jit(cholesky)/cholesky | solution.py:66
  821.3 11.7 %cholesky.415 = f32[128,128]{1,0:T(8,128)S(1)} custom-call(f32[128,128]{1,0:T(8,128)S(1)} %convolution_subtract_fusion.12), custom_call_target="Cholesky" | custom-call | tf_op jit(solution)/shard_map/jit(cholesky)/cholesky | solution.py:66
  842.3 13.9 %while.5 = (s32[]{:T(128)}, f32[512,512]{1,0:T(8,128)}, s32[4,2]{0,1:T(2,128)S(1)}, f32[4,128,128]{2,1,0:T(8,128)}, s32[]{:T(128)}) while((s32[]{:T(128)}, f32[512,512]{1,0:T(8,128)}, s32[4,2]{0,1:T(2,128)S(1)}, f32[4,128,128]{2,1,0:T(8,128)}, s32[]{:T(128)}) %tuple.138), condition=%wide.while_cond.clone, body=%wide.while_body.clone.sunk | while | flops 2 | bytes 132705 | solution.py:68
  856.2 40.7 %custom-call.34 = f32[4,128,128]{1,2,0:T(8,128)} custom-call(f32[4,128,128]{2,1,0:T(8,128)} %get-tuple-element.31), custom_call_target="InvertDiagBlocksLowerTriangular" | custom-call | tf_op jit(solution)/shard_map/jit(_solve_triangular)/triangular_solve | solution.py:68
  919.6 10.1 %all-reduce.11.cloned.1.call-done = f32[1024,1536]{1,0:T(8,128)} async-done(((f32[1024,1536]{1,0:T(8,128)}), f32[1024,1536]{1,0:T(8,128)}) %all-reduce.11.cloned.1.call-update) | async-done | bytes 6291472 | tf_op jit(solution)/shard_map/psum | solution.py:105
  929.7 15.2 %fusion.1 = f32[1024,1536]{1,0:T(8,128)S(1)} fusion(f32[1024,1536]{1,0:T(8,128)} %all-reduce.11.cloned.1.call-done, f32[512,512]{1,0:T(8,128)} %pad_maximum_fusion, f32[128,512]{1,0:T(8,128)} %copy-done.21, f32[128,512]{1,0:T(8,128)} %copy-done.19, f32[128,512]{1,0:T(8,128)} %copy-done.16, f32[128,512]{1,0:T(8,128)S(1)} %copy-done.10, ...), kind=kOutput, calls=%fused_computation.17 | convolution fusion | flops 9671016448 | bytes 15728640 | tf_op jit(solution)/shard_map/dot_general | solution.py:56
  (200 shorter events, 203.1 us)
Async XLA Ops:
  12.6 94.0 %all-to-all-start = ((s32[16,1,152]{2,1,0:T(1,128)}), s32[16,1,152]{2,1,0:T(1,128)S(1)}, u32[]{:S(2)}, u32[]{:S(2)}) async-start(s32[16,1,152]{2,1,0:T(1,128)} %all_to_all.9), calls=%async_computation | async-start | bytes 32768 | tf_op jit(solution)/shard_map/all_to_all | solution.py:100
  70.7 14.2 %copy-start = (f32[512,1536]{1,0:T(8,128)}, f32[512,1536]{1,0:T(8,128)S(1)}, u32[]{:S(2)}) copy-start(f32[512,1536]{1,0:T(8,128)S(1)} %compare_select_fusion) | copy-start | bytes 9437188
  106.6 616.1 %all-to-all-start.1 = ((f32[16,152,1536]{2,1,0:T(8,128)}), f32[16,152,1536]{2,1,0:T(8,128)}, u32[]{:S(2)}, u32[]{:S(2)}) async-start(f32[16,152,1536]{2,1,0:T(8,128)} %broadcast_select_fusion), calls=%async_computation.1 | async-start | bytes 29884416 | tf_op jit(solution)/shard_map/all_to_all | solution.py:99
  113.3 387.5 %all-reduce.7.cloned.1.call-start = ((), (), s32[]{:S(2)}) async-start(), calls=%async_computation.2 | async-start | bytes 6291456 | tf_op jit(solution)/shard_map/psum | solution.py:96
  114.0 599.5 %all-reduce.9.cloned.1.call-start = ((), (), s32[]{:S(2)}) async-start(), calls=%async_computation.3 | async-start | bytes 4194304 | tf_op jit(solution)/shard_map/psum | solution.py:13
  114.2 541.7 %copy-start.4 = (f32[512,512]{1,0:T(8,128)}, f32[512,512]{1,0:T(8,128)S(1)}, u32[]{:S(2)}) copy-start(f32[512,512]{1,0:T(8,128)S(1)} %fusion.17) | copy-start | bytes 3145732
  503.9 22.7 %copy-start.18 = (f32[512,512]{1,0:T(8,128)}, f32[512,512]{1,0:T(8,128)S(1)}, u32[]{:S(2)}) copy-start(f32[512,512]{1,0:T(8,128)S(1)} %fusion.14) | copy-start | bytes 3145732
  527.6 121.8 %slice-start = ((f32[512,1536]{1,0:T(8,128)}), f32[512,1024]{1,0:T(8,128)S(1)}, s32[]{:S(2)}) async-start(f32[512,1536]{1,0:T(8,128)} %copy-done), calls=%async_computation.6 | async-start | bytes 4194304 | tf_op jit(solution)/shard_map/slice | solution.py:89
  650.9 260.7 %all-reduce.13.cloned.1.call-start = ((), (), s32[]{:S(2)}) async-start(), calls=%async_computation.5 | async-start | bytes 4194304 | tf_op jit(solution)/shard_map/psum | solution.py:13
  650.9 7.1 copy-start.13
  654.0 7.6 copy-start.6
  655.9 5.8 copy-start.11
  662.7 50.9 %copy-start.1 = (f32[512,1536]{1,0:T(8,128)S(1)}, f32[512,1536]{1,0:T(8,128)}, u32[]{:S(2)}) copy-start(f32[512,1536]{1,0:T(8,128)} %copy-done) | copy-start | bytes 9437188
  736.4 193.3 %all-reduce.11.cloned.1.call-start = ((), (), s32[]{:S(2)}) async-start(), calls=%async_computation.4 | async-start | bytes 12582912 | tf_op jit(solution)/shard_map/psum | solution.py:105
  897.0 5.4 copy-start.24
  897.0 5.8 copy-start.5
  899.2 7.6 copy-start.3
  899.2 7.6 copy-start.7
  899.2 7.6 copy-start.12
  899.2 7.6 copy-start.15
  900.8 7.9 copy-start.9
  902.8 5.9 copy-start.16
  911.6 18.1 %copy-start.10 = (f32[128,512]{1,0:T(8,128)S(1)}, f32[128,512]{1,0:T(8,128)}, u32[]{:S(2)}) copy-start(f32[128,512]{1,0:T(8,128)} %copy-done.9) | copy-start | bytes 786436
  929.7 15.2 %copy-start.20 = (f32[512,1024]{1,0:T(8,128)S(1)}, f32[512,1024]{1,0:T(8,128)}, u32[]{:S(2)}) copy-start(f32[512,1024]{1,0:T(8,128)} %fusion) | copy-start | bytes 6291460
  (8 other events, 16.9 us)
Sparse Core Ops, SparseCore 0:
  118.9 381.9 all-reduce.6
  651.0 62.4 all-reduce.8
  736.5 65.7 all-reduce.12
  806.0 123.6 all-reduce.10
where the time goes:
time: 972 us; the launch traced here: 960 us
  waiting for transfers between devices  430 us (44%)
  other arithmetic  320 us (33%)
  matrix products  89.4 us (9%)
  local copies, waits for them, and re-layouts  85.2 us (9%)
  between operations  20 us (2%)
  starting transfers between devices  14.6 us (2%)
    psum x1, waiting for transfers between devices, shards(): gram = lax.psum(gram, ('gr', 'gc'))  374 us
    another operation x29, other arithmetic, cholesky_inverse(): lower = jnp.linalg.cholesky(gram)  166 us
    another operation x6, other arithmetic, cholesky_inverse(): return jax.scipy.linalg.solve_triangular(lower, eye, lower=True)  87.6 us
    psum x2, waiting for transfers between devices, spread(): return lax.psum(kept, axis)  45.4 us
    select_n x1, other arithmetic, shards(): limits = jnp.take(stair, row_map // STAIR_BLOCK)  40.5 us
    dot_general x4, matrix products, high(): lax.dot_general(left, right, (contract, ((), ())), precision=lax.Precisio...  39.7 us
    another operation x27, local copies, waits for them, and re-layouts, cholesky_inverse(): return jax.scipy.linalg.solve_triangular(lower, eye, lower=True)  26 us
  transfers between devices with their start and end apart: 6, of which 3 were waited for; matrix products, arithmetic and copies ran while one was open for 47% of the time, Pallas kernels for 0%

commit v1 on v0

--- a/solution.py
+++ b/solution.py
@@ -93,7 +93,7 @@
     gram = jnp.concatenate([left, low], axis=1)
     gram = jnp.where(lax.axis_index("gc") == 0, gram, jnp.zeros_like(gram))
     gram, masked, own = lax.optimization_barrier((gram, masked, own))
-    gram = lax.psum(gram, ("gr", "gc"))
+    gram = lax.psum(lax.psum(gram, "gc"), "gr")
     sent_rows, sent_slots = pack_rows(masked, row_map, groups)
     recv_rows, recv_slots = (
         lax.all_to_all(sent_rows, "gr", split_axis=0, concat_axis=0, tiled=True),

time: 972 us -> 907 us (0.933)
  waiting for transfers between devices: 430 us -> 365 us
    psum x1 -> x2, waiting for transfers between devices: 374 us -> 308 us  [shards(): gram = lax.psum(lax.psum(gram, 'gc'), 'gr')]
  transfers between devices with their start and end apart: 6 -> 7, of which waited for: 3 -> 4; matrix products, arithmetic and copies ran while one was open for 47% -> 50% of each run, Pallas kernels for 0% -> 0%
where the time goes in v1:
time: 907 us; the launch traced here: 895 us
  waiting for transfers between devices  365 us (40%)
  other arithmetic  320 us (35%)
  matrix products  89.4 us (10%)
  local copies, waits for them, and re-layouts  85.2 us (9%)
  between operations  20 us (2%)
  starting transfers between devices  14.7 us (2%)
    psum x2, waiting for transfers between devices, shards(): gram = lax.psum(lax.psum(gram, 'gc'), 'gr')  308 us
    another operation x29, other arithmetic, cholesky_inverse(): lower = jnp.linalg.cholesky(gram)  166 us
    another operation x6, other arithmetic, cholesky_inverse(): return jax.scipy.linalg.solve_triangular(lower, eye, lower=True)  87.6 us
    psum x2, waiting for transfers between devices, spread(): return lax.psum(kept, axis)  46.4 us
    select_n x1, other arithmetic, shards(): limits = jnp.take(stair, row_map // STAIR_BLOCK)  40.5 us
    dot_general x4, matrix products, high(): lax.dot_general(left, right, (contract, ((), ())), precision=lax.Precisio...  39.7 us
    another operation x27, local copies, waits for them, and re-layouts, cholesky_inverse(): return jax.scipy.linalg.solve_triangular(lower, eye, lower=True)  26 us
    dot_general x6, matrix products, matmul(): jnp.dot(left, right, precision=lax.Precision.HIGHEST, preferred_element_t...  18.9 us
  transfers between devices with their start and end apart: 7, of which 4 were waited for; matrix products, arithmetic and copies ran while one was open for 50% of the time, Pallas kernels for 0%

profile of v1, /device:TPU:1, one launch (start us, length us, event | category | flops | bytes accessed | tf_op | source)
XLA Modules:
  0.0 895.0 jit_solution(11313348866431716438)
XLA Ops:
  28.0 40.5 %select_select_fusion.2 = s32[512]{0:T(512)S(1)} fusion(s32[512]{0:T(512)} %param.7, s32[]{:T(128)} %bitcast, s32[]{:T(128)} %bitcast.1, s32[]{:T(128)} %bitcast.2, s32[]{:T(128)} %bitcast.3, s32[]{:T(128)} %bitcast.4, s32[]{:T(128)} %bitcast.5, s32[]{:T(128)} %bitcast.6, s32[]{:T(128)} %bitcast.7, s32[]{:T(128)} %bitcast.8, s32[]{:T(128)} %bitcast.9, ...), kind=kLoop, calls=%fused_computation.171 | loop fusion | flops 75776 | bytes 4352 | tf_op jit(solution)/shard_map/jit(_take)/select_n | solution.py:87
  84.9 10.1 %gather_fusion = f32[2432,1536]{1,0:T(8,128)} fusion(f32[512,1536]{1,0:T(8,128)S(1)} %compare_select_fusion, s32[3072]{0:T(1024)S(1)} %pad_clamp_fusion), kind=kCustom, calls=%fused_computation | custom fusion | bytes 29894144 | tf_op jit(solution)/shard_map/jit(_take)/gather | solution.py:30
  95.0 11.6 %broadcast_select_fusion = f32[16,152,1536]{2,1,0:T(8,128)} fusion(f32[16,152,1536]{2,1,0:T(8,128)} %bitcast.192, pred[16,152]{1,0:T(8,128)(4,1)S(1)} %broadcast_in_dim.63), kind=kLoop, calls=%fused_computation.9 | loop fusion | flops 3735552 | bytes 29886848 | tf_op jit(solution)/shard_map/jit(_take)/select_n | solution.py:30
  114.1 74.6 %all-reduce.8.cloned.1.call-done = f32[1024,768]{0,1:T(8,128)} async-done(((f32[1024,768]{0,1:T(8,128)}), f32[1024,768]{0,1:T(8,128)}) %all-reduce.8.cloned.1.call-update) | async-done | bytes 3145744 | tf_op jit(solution)/shard_map/psum | solution.py:96
  189.1 12.8 %scatter_custom_fusion.1 = s32[512]{0:T(512)S(1)} fusion(s32[2432]{0:T(1024)S(1)} %fusion.76, s32[2432]{0:T(1024)S(1)} %iota.96, s32[]{:T(128)} %copy.56), kind=kCustom, calls=%fused_computation.190 | custom fusion | bytes 2052 | tf_op jit(solution)/shard_map/scatter | solution.py:46
  202.0 233.3 %all-reduce.10.cloned.1.call-done = f32[1024,768]{0,1:T(8,128)} async-done(((f32[1024,768]{0,1:T(8,128)}), f32[1024,768]{0,1:T(8,128)}) %all-reduce.10.cloned.1.call-update) | async-done | bytes 3145744 | tf_op jit(solution)/shard_map/psum | solution.py:96
  438.4 11.7 %cholesky.286 = f32[128,128]{1,0:T(8,128)S(1)} custom-call(f32[128,128]{1,0:T(8,128)S(1)} %cholesky.426), custom_call_target="Cholesky" | custom-call | tf_op jit(solution)/shard_map/jit(cholesky)/cholesky | solution.py:66
  463.5 11.7 %cholesky.305 = f32[128,128]{1,0:T(8,128)S(1)} custom-call(f32[128,128]{1,0:T(8,128)S(1)} %cholesky.430), custom_call_target="Cholesky" | custom-call | tf_op jit(solution)/shard_map/jit(cholesky)/cholesky | solution.py:66
  475.9 10.0 %custom-call.28 = f32[1,128,128]{1,2,0:T(8,128)S(1)} custom-call(f32[1,128,128]{2,1,0:T(8,128)S(1)} %get-tuple-element.72), custom_call_target="InvertDiagBlocksLowerTriangular" | custom-call | tf_op jit(solution)/shard_map/jit(cholesky)/cholesky | solution.py:66
  488.2 11.7 %cholesky.326 = f32[128,128]{1,0:T(8,128)S(1)} custom-call(f32[128,128]{1,0:T(8,128)S(1)} %cholesky.435), custom_call_target="Cholesky" | custom-call | tf_op jit(solution)/shard_map/jit(cholesky)/cholesky | solution.py:66
  512.6 11.7 %cholesky.343 = f32[128,128]{1,0:T(8,128)S(1)} custom-call(f32[128,128]{1,0:T(8,128)S(1)} %convolution_subtract_fusion.13), custom_call_target="Cholesky" | custom-call | tf_op jit(solution)/shard_map/jit(cholesky)/cholesky | solution.py:66
  532.1 11.8 %while.4 = (s32[]{:T(128)}, f32[512,512]{1,0:T(8,128)}, s32[4,2]{0,1:T(2,128)S(1)}, f32[4,128,128]{2,1,0:T(8,128)S(1)}, s32[]{:T(128)}) while((s32[]{:T(128)}, f32[512,512]{1,0:T(8,128)}, s32[4,2]{0,1:T(2,128)S(1)}, f32[4,128,128]{2,1,0:T(8,128)S(1)}, s32[]{:T(128)}) %tuple.124), condition=%wide.while_cond, body=%wide.while_body.sunk | while | flops 2 | bytes 131181 | solution.py:68
  543.9 39.9 %custom-call.30 = f32[4,128,128]{1,2,0:T(8,128)} custom-call(f32[4,128,128]{2,1,0:T(8,128)S(1)} %get-tuple-element.30), custom_call_target="InvertDiagBlocksLowerTriangular" | custom-call | tf_op jit(solution)/shard_map/jit(_solve_triangular)/triangular_solve | solution.py:68
  602.6 46.4 %all-reduce.12.cloned.1.call-done = f32[512,1024]{1,0:T(8,128)} async-done(((f32[512,1024]{1,0:T(8,128)}), f32[512,1024]{1,0:T(8,128)}) %all-reduce.12.cloned.1.call-update) | async-done | bytes 2097168 | tf_op jit(solution)/shard_map/psum | solution.py:13
  674.9 11.7 %cholesky.358 = f32[128,128]{1,0:T(8,128)S(1)} custom-call(f32[128,128]{1,0:T(8,128)S(1)} %cholesky.439), custom_call_target="Cholesky" | custom-call | tf_op jit(solution)/shard_map/jit(cholesky)/cholesky | solution.py:66
  701.5 11.7 %cholesky.377 = f32[128,128]{1,0:T(8,128)S(1)} custom-call(f32[128,128]{1,0:T(8,128)S(1)} %cholesky.443), custom_call_target="Cholesky" | custom-call | tf_op jit(solution)/shard_map/jit(cholesky)/cholesky | solution.py:66
  713.8 10.0 %custom-call.32 = f32[1,128,128]{1,2,0:T(8,128)S(1)} custom-call(f32[1,128,128]{2,1,0:T(8,128)S(1)} %get-tuple-element.62), custom_call_target="InvertDiagBlocksLowerTriangular" | custom-call | tf_op jit(solution)/shard_map/jit(cholesky)/cholesky | solution.py:66
  727.8 13.2 %cholesky.398 = f32[128,128]{1,0:T(8,128)} custom-call(f32[128,128]{1,0:T(8,128)} %cholesky.448), custom_call_target="Cholesky" | custom-call | tf_op jit(solution)/shard_map/jit(cholesky)/cholesky | solution.py:66
  742.4 11.3 %custom-call.33 = f32[1,128,128]{1,2,0:T(8,128)} custom-call(f32[1,128,128]{2,1,0:T(8,128)} %get-tuple-element.59), custom_call_target="InvertDiagBlocksLowerTriangular" | custom-call | tf_op jit(solution)/shard_map/jit(cholesky)/cholesky | solution.py:66
  756.8 11.7 %cholesky.415 = f32[128,128]{1,0:T(8,128)S(1)} custom-call(f32[128,128]{1,0:T(8,128)S(1)} %convolution_subtract_fusion.12), custom_call_target="Cholesky" | custom-call | tf_op jit(solution)/shard_map/jit(cholesky)/cholesky | solution.py:66
  777.8 13.9 %while.5 = (s32[]{:T(128)}, f32[512,512]{1,0:T(8,128)}, s32[4,2]{0,1:T(2,128)S(1)}, f32[4,128,128]{2,1,0:T(8,128)}, s32[]{:T(128)}) while((s32[]{:T(128)}, f32[512,512]{1,0:T(8,128)}, s32[4,2]{0,1:T(2,128)S(1)}, f32[4,128,128]{2,1,0:T(8,128)}, s32[]{:T(128)}) %tuple.140), condition=%wide.while_cond.clone, body=%wide.while_body.clone.sunk | while | flops 2 | bytes 132705 | solution.py:68
  791.7 40.7 %custom-call.34 = f32[4,128,128]{1,2,0:T(8,128)} custom-call(f32[4,128,128]{2,1,0:T(8,128)} %get-tuple-element.31), custom_call_target="InvertDiagBlocksLowerTriangular" | custom-call | tf_op jit(solution)/shard_map/jit(_solve_triangular)/triangular_solve | solution.py:68
  855.1 10.0 %all-reduce.14.cloned.1.call-done = f32[1024,1536]{1,0:T(8,128)} async-done(((f32[1024,1536]{1,0:T(8,128)}), f32[1024,1536]{1,0:T(8,128)}) %all-reduce.14.cloned.1.call-update) | async-done | bytes 6291472 | tf_op jit(solution)/shard_map/psum | solution.py:105
  865.1 15.2 %fusion.1 = f32[1024,1536]{1,0:T(8,128)S(1)} fusion(f32[1024,1536]{1,0:T(8,128)} %all-reduce.14.cloned.1.call-done, f32[512,512]{1,0:T(8,128)} %pad_maximum_fusion, f32[128,512]{1,0:T(8,128)} %copy-done.21, f32[128,512]{1,0:T(8,128)} %copy-done.19, f32[128,512]{1,0:T(8,128)} %copy-done.16, f32[128,512]{1,0:T(8,128)S(1)} %copy-done.10, ...), kind=kOutput, calls=%fused_computation.17 | convolution fusion | flops 9671016448 | bytes 15728640 | tf_op jit(solution)/shard_map/dot_general | solution.py:56
  (203 shorter events, 213.0 us)
Async XLA Ops:
  12.6 94.1 %all-to-all-start = ((s32[16,1,152]{2,1,0:T(1,128)}), s32[16,1,152]{2,1,0:T(1,128)S(1)}, u32[]{:S(2)}, u32[]{:S(2)}) async-start(s32[16,1,152]{2,1,0:T(1,128)} %all_to_all.9), calls=%async_computation | async-start | bytes 32768 | tf_op jit(solution)/shard_map/all_to_all | solution.py:100
  70.7 14.2 %copy-start = (f32[512,1536]{1,0:T(8,128)}, f32[512,1536]{1,0:T(8,128)S(1)}, u32[]{:S(2)}) copy-start(f32[512,1536]{1,0:T(8,128)S(1)} %compare_select_fusion) | copy-start | bytes 9437188
  106.6 551.6 %all-to-all-start.1 = ((f32[16,152,1536]{2,1,0:T(8,128)}), f32[16,152,1536]{2,1,0:T(8,128)}, u32[]{:S(2)}, u32[]{:S(2)}) async-start(f32[16,152,1536]{2,1,0:T(8,128)} %broadcast_select_fusion), calls=%async_computation.1 | async-start | bytes 29884416 | tf_op jit(solution)/shard_map/all_to_all | solution.py:99
  113.3 75.4 %all-reduce.8.cloned.1.call-start = ((), (), s32[]{:S(2)}) async-start(), calls=%async_computation.2 | async-start | bytes 6291456 | tf_op jit(solution)/shard_map/psum | solution.py:96
  114.1 321.2 %all-reduce.10.cloned.1.call-start = ((), (), s32[]{:S(2)}) async-start(), calls=%async_computation.3 | async-start | bytes 6291456 | tf_op jit(solution)/shard_map/psum | solution.py:96
  188.7 460.3 %all-reduce.12.cloned.1.call-start = ((), (), s32[]{:S(2)}) async-start(), calls=%async_computation.4 | async-start | bytes 4194304 | tf_op jit(solution)/shard_map/psum | solution.py:13
  188.9 401.4 %copy-start.4 = (f32[512,512]{1,0:T(8,128)}, f32[512,512]{1,0:T(8,128)S(1)}, u32[]{:S(2)}) copy-start(f32[512,512]{1,0:T(8,128)S(1)} %fusion.17) | copy-start | bytes 3145732
  438.4 22.7 %copy-start.18 = (f32[512,512]{1,0:T(8,128)}, f32[512,512]{1,0:T(8,128)S(1)}, u32[]{:S(2)}) copy-start(f32[512,512]{1,0:T(8,128)S(1)} %fusion.14) | copy-start | bytes 3145732
  462.1 121.8 %slice-start = ((f32[512,1536]{1,0:T(8,128)}), f32[512,1024]{1,0:T(8,128)S(1)}, s32[]{:S(2)}) async-start(f32[512,1536]{1,0:T(8,128)} %copy-done), calls=%async_computation.7 | async-start | bytes 4194304 | tf_op jit(solution)/shard_map/slice | solution.py:89
  585.4 261.7 %all-reduce.16.cloned.1.call-start = ((), (), s32[]{:S(2)}) async-start(), calls=%async_computation.6 | async-start | bytes 4194304 | tf_op jit(solution)/shard_map/psum | solution.py:13
  585.4 7.1 copy-start.13
  588.5 7.7 copy-start.6
  590.4 5.8 copy-start.11
  597.1 51.9 %copy-start.1 = (f32[512,1536]{1,0:T(8,128)S(1)}, f32[512,1536]{1,0:T(8,128)}, u32[]{:S(2)}) copy-start(f32[512,1536]{1,0:T(8,128)} %copy-done) | copy-start | bytes 9437188
  671.9 193.2 %all-reduce.14.cloned.1.call-start = ((), (), s32[]{:S(2)}) async-start(), calls=%async_computation.5 | async-start | bytes 12582912 | tf_op jit(solution)/shard_map/psum | solution.py:105
  832.5 5.8 copy-start.5
  834.8 7.6 copy-start.3
  834.8 7.6 copy-start.7
  834.8 7.6 copy-start.12
  834.8 7.6 copy-start.15
  836.4 7.9 copy-start.9
  838.3 5.9 copy-start.16
  847.1 18.0 %copy-start.10 = (f32[128,512]{1,0:T(8,128)S(1)}, f32[128,512]{1,0:T(8,128)}, u32[]{:S(2)}) copy-start(f32[128,512]{1,0:T(8,128)} %copy-done.9) | copy-start | bytes 786436
  865.1 15.2 %copy-start.20 = (f32[512,1024]{1,0:T(8,128)S(1)}, f32[512,1024]{1,0:T(8,128)}, u32[]{:S(2)}) copy-start(f32[512,1024]{1,0:T(8,128)} %fusion) | copy-start | bytes 6291460
  (9 other events, 22.3 us)
Sparse Core Ops, SparseCore 0:
  116.5 72.1 all-reduce.7
  192.1 243.1 all-reduce.9
  585.5 63.5 all-reduce.11
  672.1 65.7 all-reduce.15
  741.1 123.9 all-reduce.13
